TPU v7x, 256 devices: a whole 4x4x8 slice. The times are simulated.
256 devices in a mesh: snap: 16 (over z, y_lo), space: 16 (over x, y_hi, core).
Axes of the slice: x: 4, y: 4 (y_hi: 2, y_lo: 2; y = y_hi * 2 + y_lo), z: 8, core: 2. Of those that a mesh axis runs over, the one named last changes fastest.
Arguments:
- snapshots: bfloat16 [2048, 2, 64, 720], P('snap', None, 'space'), may hold values from -6 to 6
- lon_coeff: float32 [2, 64, 720], P(None, 'space'), may hold values from 0.05 to 0.24
- lat_coeff: float32 [2, 64, 720], P(None, 'space'), may hold values from 0.1 to 0.24
Outputs:
- gram: float32 [2048, 2048], P('snap', 'space')
All inputs are finite; a program needn't handle non-finite values.
Results may differ from a plain program's by a relative error of at most 0.00062.
Values may be sent and summed in bfloat16 or wider, within the bound.
A program may use at most 128 MiB of HBM per device.

v0:
```python
import math
import jax
import jax.numpy as jnp
from jax import lax
from jax.sharding import PartitionSpec as P


def padded_2(cells, sides, width):
    for axis, dim in sides:
        count = lax.axis_size(axis)
        ends = count - 1
        head = lax.slice_in_dim(cells, 0, width, axis=dim)
        tail = lax.slice_in_dim(cells, cells.shape[dim] - width, cells.shape[dim], axis=dim)
        cells = jnp.concatenate(
            [
                lax.ppermute(tail, axis, [(i, (i + 1) % count) for i in range(ends)]),
                cells,
                lax.ppermute(head, axis, [((i + 1) % count, i) for i in range(ends)]),
            ],
            axis=dim,
        )
    return cells


def inner_tile(left, right):
    return lax.dot_general(
        left, right, (((1,), (1,)), ((), ())), preferred_element_type=jnp.float32
    )


def shards(snapshots, lon_coeff, lat_coeff):
    snap_rows, fields, rows, nlon = snapshots.shape
    bands = lax.axis_size("space")
    padded = padded_2(snapshots, (("space", 2),), 1).astype(jnp.float32)
    values = snapshots.astype(jnp.float32)
    lon_part = jnp.roll(values, 1, axis=3) + jnp.roll(values, -1, axis=3) - 2.0 * values
    lat_part = padded[:, :, 2:] + padded[:, :, :-2] - 2.0 * values
    smooth = values + lon_coeff * lon_part + lat_coeff * lat_part
    nlat = bands * rows
    every_row = jnp.arange(nlat).astype(jnp.float32)
    every_cos = jnp.cos((45.0 + 0.5 * (every_row + 0.5 - nlat / 2.0)) * (math.pi / 180.0))
    total = fields * nlon * jnp.sum(every_cos)
    my_rows = (lax.axis_index("space") * rows + jnp.arange(rows)).astype(jnp.float32)
    cosine = jnp.cos((45.0 + 0.5 * (my_rows + 0.5 - nlat / 2.0)) * (math.pi / 180.0))
    factor = jnp.sqrt(cosine) * total ** (-0.25)
    scaled = (smooth * factor[:, None]).astype(jnp.bfloat16).reshape(snap_rows, -1)
    partial_value = inner_tile(scaled, lax.all_gather(scaled, "snap", axis=0, tiled=True))
    return lax.psum_scatter(partial_value, "space", scatter_dimension=1, tiled=True)


def solution(mesh):
    return jax.shard_map(
        shards,
        mesh=mesh,
        in_specs=(P("snap", None, "space", None), P(None, "space", None), P(None, "space", None)),
        out_specs=P("snap", "space"),
        check_vma=False,
    )
```

profile of v0, /device:TPU:2, one launch (start us, length us, event | category | flops | bytes accessed | tf_op | source)
XLA Modules:
  0.0 613.8 jit_solution(12110628258936550416)
XLA Ops:
  6.5 0.0 copy-start
  6.5 0.0 all-gather.2.cloned.1.call-start
  6.5 1.3 fusion.10
  7.8 1.9 collective-permute-start
  9.7 6.0 collective-permute-start.1
  15.8 0.6 cosine_reduce_fusion
  16.4 0.7 fusion.9
  17.9 0.1 sqrt_multiply_fusion
  17.9 0.0 copy-done
  17.9 0.4 fusion.8
  18.3 0.0 copy-start.1
  18.3 0.0 copy-start.2
  18.4 0.7 collective-permute-done
  19.0 1.8 collective-permute-done.1
  20.8 0.3 maximum_convert_fusion
  21.1 0.0 copy-done.1
  21.1 0.0 copy-done.2
  21.2 3.9 fusion.4
  25.1 0.0 all-gather.2.cloned.1.call-update
  25.1 0.0 reduce-scatter.2.cloned.1.call-start
  25.1 493.8 %all-gather.2.cloned.1.call-done = bf16[2048,5760]{0,1:T(8,128)(2,1)} async-done(((bf16[128,5760]{0,1:T(8,128)(2,1)}), bf16[2048,5760]{0,1:T(8,128)(2,1)}) %all-gather.2.cloned.1.call-update) | async-done | bytes 23592976 | tf_op jit(solution)/shard_map/all_gather | solution.py:47
  518.9 12.5 %fusion.11 = f32[128,2048]{1,0:T(8,128)} fusion(bf16[128,5760]{0,1:T(8,128)(2,1)} %bitcast.4, bf16[2048,5760]{0,1:T(8,128)(2,1)} %all-gather.2.cloned.1.call-done), kind=kOutput, calls=%fused_computation.16 | convolution fusion | flops 3019898880 | bytes 26116096 | tf_op jit(solution)/shard_map/dot_general | solution.py:26
  531.4 0.0 reduce-scatter.2.cloned.1.call-update
  531.5 75.5 %reduce-scatter.2.cloned.1.call-done = f32[128,128]{1,0:T(8,128)} async-done(((f32[128,2048]{1,0:T(8,128)}), f32[128,128]{1,0:T(8,128)}) %reduce-scatter.2.cloned.1.call-update) | async-done | bytes 65552 | tf_op jit(solution)/shard_map/reduce_scatter | solution.py:48
Async XLA Ops:
  6.5 11.4 %copy-start = (bf16[128,2,4,720]{0,3,2,1:T(8,128)(2,1)S(1)}, bf16[128,2,4,720]{0,3,2,1:T(8,128)(2,1)}, u32[]{:S(2)}) copy-start(bf16[128,2,4,720]{0,3,2,1:T(8,128)(2,1)} %param.3) | copy-start | bytes 4423684
  6.5 512.4 %all-gather.2.cloned.1.call-start = ((), (), s32[]{:S(2)}) async-start(), calls=%async_computation.1 | async-start | bytes 25067520 | tf_op jit(solution)/shard_map/all_gather | solution.py:47
  7.8 11.2 %collective-permute-start = (bf16[128,2,1,720]{0,3,2,1:T(8,128)(2,1)S(1)}, bf16[128,2,1,720]{0,3,2,1:T(8,128)(2,1)S(1)}, u32[]{:S(2)}, u32[]{:S(2)}) collective-permute-start(bf16[128,2,1,720]{0,3,2,1:T(8,128)(2,1)S(1)} %get-tuple-element.9), channel_id=1, source_target_pairs={{0,1},{1,2},{2,3},{3,4},{4,5},{5,6},{6,7},{7,8},{8,9},{9,10},{10,1... | collective-permute-start | bytes 1105928 | tf_op jit(solution)/shard_map/ppermute | solution.py:16
  9.7 11.1 %collective-permute-start.1 = (bf16[128,2,1,720]{0,3,2,1:T(8,128)(2,1)S(1)}, bf16[128,2,1,720]{0,3,2,1:T(8,128)(2,1)S(1)}, u32[]{:S(2)}, u32[]{:S(2)}) collective-permute-start(bf16[128,2,1,720]{0,3,2,1:T(8,128)(2,1)S(1)} %get-tuple-element.10), channel_id=1, source_target_pairs={{1,0},{2,1},{3,2},{4,3},{5,4},{6,5},{7,6},{8,7},{9,8},{10,9},{11,1... | collective-permute-start | bytes 1105928 | tf_op jit(solution)/shard_map/ppermute | solution.py:18
  18.3 2.8 copy-start.1
  18.3 2.8 copy-start.2
  25.1 581.8 %reduce-scatter.2.cloned.1.call-start = ((), (), s32[]{:S(2)}) async-start(), calls=%async_computation.2 | async-start | bytes 1114112 | tf_op jit(solution)/shard_map/reduce_scatter | solution.py:48
Sparse Core Ops, SparseCore 0:
  25.2 493.6 all-gather.1
  531.6 75.2 reduce-scatter.1
where the time goes:
time: 614 us
  waiting for transfers between devices  572 us (93%)
  between operations  14.2 us (2%)
  matrix products  12.5 us (2%)
  starting transfers between devices  8.01 us (1%)
    all_gather x1, waiting for transfers between devices, shards(): lax.all_gather(scaled, 'snap', axis=0, tiled=True)  494 us
    reduce_scatter x1, waiting for transfers between devices, shards(): lax.psum_scatter(partial_value, 'space', scatter_dimension=1, tiled=True)  75.5 us
    dot_general x1, matrix products, inner_tile(): lax.dot_general(left, right, (((1,), (1,)), ((), ())), preferred_element_...  12.5 us
  transfers between devices with their start and end apart: 4, of which 4 were waited for; matrix products, arithmetic and copies ran while one was open for 0% of the time, Pallas kernels for 0%

commit v1 on v0

--- a/solution.py
+++ b/solution.py
@@ -29,6 +29,13 @@
 
 
 def shards(snapshots, lon_coeff, lat_coeff):
+
+    def remake_vectors(m):
+        formed = lax.axis_size("snap")
+        o_now = jnp.stack([m] * formed, axis=0)
+        block_now = lax.all_to_all(o_now, "snap", 0, 0)
+        return jnp.concatenate(block_now, axis=0)
+
     snap_rows, fields, rows, nlon = snapshots.shape
     bands = lax.axis_size("space")
     padded = padded_2(snapshots, (("space", 2),), 1).astype(jnp.float32)
@@ -44,7 +51,7 @@
     cosine = jnp.cos((45.0 + 0.5 * (my_rows + 0.5 - nlat / 2.0)) * (math.pi / 180.0))
     factor = jnp.sqrt(cosine) * total ** (-0.25)
     scaled = (smooth * factor[:, None]).astype(jnp.bfloat16).reshape(snap_rows, -1)
-    partial_value = inner_tile(scaled, lax.all_gather(scaled, "snap", axis=0, tiled=True))
+    partial_value = inner_tile(scaled, remake_vectors(scaled))
     return lax.psum_scatter(partial_value, "space", scatter_dimension=1, tiled=True)
 
 

time: 614 us -> 642 us (1.046)
  blocking collectives: 0 us -> 521 us
  waiting for transfers between devices: 572 us -> 74.4 us
    all_to_all x0 -> x1, blocking collectives: none -> 521 us  [remake_vectors(): block_now = lax.all_to_all(o_now, 'snap', 0, 0)]
    all_gather x1 -> x0, waiting for transfers between devices: 494 us -> none  [shards(): lax.all_gather(scaled, 'snap', axis=0, tiled=True)]
  transfers between devices with their start and end apart: 4 -> 3, of which waited for: 4 -> 3; matrix products, arithmetic and copies ran while one was open for 0% -> 0% of each run, Pallas kernels for 0% -> 0%
where the time goes in v1:
time: 642 us
  blocking collectives  521 us (81%)
  waiting for transfers between devices  74.4 us (12%)
  between operations  14.2 us (2%)
  matrix products  13.5 us (2%)
  starting transfers between devices  7.97 us (1%)
  local copies, waits for them, and re-layouts  6.43 us (1%)
    all_to_all x1, blocking collectives, remake_vectors(): block_now = lax.all_to_all(o_now, 'snap', 0, 0)  521 us
    reduce_scatter x1, waiting for transfers between devices, shards(): lax.psum_scatter(partial_value, 'space', scatter_dimension=1, tiled=True)  71.9 us
    dot_general x1, matrix products, inner_tile(): lax.dot_general(left, right, (((1,), (1,)), ((), ())), preferred_element_...  13.5 us
  transfers between devices with their start and end apart: 3, of which 3 were waited for; matrix products, arithmetic and copies ran while one was open for 0% of the time, Pallas kernels for 0%

profile of v1, /device:TPU:2, one launch (start us, length us, event | category | flops | bytes accessed | tf_op | source)
XLA Modules:
  0.0 641.9 jit_solution(13279693279802496060)
XLA Ops:
  6.5 0.0 copy-start
  6.5 0.0 reduce-scatter.2.cloned.1.call-start
  6.5 1.3 fusion.10
  7.8 1.9 collective-permute-start
  9.7 6.0 collective-permute-start.1
  15.8 0.6 cosine_reduce_fusion
  16.4 0.7 fusion.9
  17.9 0.1 sqrt_multiply_fusion
  17.9 0.0 copy-done
  17.9 0.4 fusion.8
  18.3 0.0 copy-start.1
  18.3 0.0 copy-start.2
  18.4 0.7 collective-permute-done
  19.0 1.8 collective-permute-done.1
  20.8 0.3 maximum_convert_fusion
  21.1 0.0 copy-done.1
  21.1 0.0 copy-done.2
  21.2 3.1 fusion.4
  24.2 1.5 copy.4
  25.7 2.6 stack.3
  28.3 521.3 %all_to_all.5 = bf16[16,128,5760]{2,1,0:T(8,128)(2,1)} all-to-all(bf16[16,128,5760]{2,1,0:T(8,128)(2,1)S(1)} %stack.3), channel_id=1, replica_groups=mesh['snap'=16,'space'=16] {'snap'}, dimensions={0} | all-to-all | bytes 47185920 | tf_op jit(solution)/shard_map/all_to_all | solution.py:36
  549.6 13.5 %fusion.11 = f32[128,2048]{1,0:T(8,128)} fusion(bf16[128,5760]{0,1:T(8,128)(2,1)S(1)} %bitcast.6, bf16[2048,5760]{1,0:T(8,128)(2,1)} %bitcast.4), kind=kOutput, calls=%fused_computation.16 | convolution fusion | flops 3019898880 | bytes 26116096 | tf_op jit(solution)/shard_map/dot_general | solution.py:26
  563.1 0.0 reduce-scatter.2.cloned.1.call-update
  563.1 71.9 %reduce-scatter.2.cloned.1.call-done = f32[128,128]{1,0:T(8,128)} async-done(((f32[128,2048]{1,0:T(8,128)}), f32[128,128]{1,0:T(8,128)}) %reduce-scatter.2.cloned.1.call-update) | async-done | bytes 65552 | tf_op jit(solution)/shard_map/reduce_scatter | solution.py:55
Async XLA Ops:
  6.5 11.4 %copy-start = (bf16[128,2,4,720]{0,3,2,1:T(8,128)(2,1)S(1)}, bf16[128,2,4,720]{0,3,2,1:T(8,128)(2,1)}, u32[]{:S(2)}) copy-start(bf16[128,2,4,720]{0,3,2,1:T(8,128)(2,1)} %param.3) | copy-start | bytes 4423684
  6.5 628.5 %reduce-scatter.2.cloned.1.call-start = ((), (), s32[]{:S(2)}) async-start(), calls=%async_computation.2 | async-start | bytes 1114112 | tf_op jit(solution)/shard_map/reduce_scatter | solution.py:55
  7.8 11.2 %collective-permute-start = (bf16[128,2,1,720]{0,3,2,1:T(8,128)(2,1)S(1)}, bf16[128,2,1,720]{0,3,2,1:T(8,128)(2,1)S(1)}, u32[]{:S(2)}, u32[]{:S(2)}) collective-permute-start(bf16[128,2,1,720]{0,3,2,1:T(8,128)(2,1)S(1)} %get-tuple-element.9), channel_id=1, source_target_pairs={{0,1},{1,2},{2,3},{3,4},{4,5},{5,6},{6,7},{7,8},{8,9},{9,10},{10,1... | collective-permute-start | bytes 1105928 | tf_op jit(solution)/shard_map/ppermute | solution.py:16
  9.7 11.1 %collective-permute-start.1 = (bf16[128,2,1,720]{0,3,2,1:T(8,128)(2,1)S(1)}, bf16[128,2,1,720]{0,3,2,1:T(8,128)(2,1)S(1)}, u32[]{:S(2)}, u32[]{:S(2)}) collective-permute-start(bf16[128,2,1,720]{0,3,2,1:T(8,128)(2,1)S(1)} %get-tuple-element.10), channel_id=1, source_target_pairs={{1,0},{2,1},{3,2},{4,3},{5,4},{6,5},{7,6},{8,7},{9,8},{10,9},{11,1... | collective-permute-start | bytes 1105928 | tf_op jit(solution)/shard_map/ppermute | solution.py:18
  18.3 2.8 copy-start.1
  18.3 2.8 copy-start.2
Sparse Core Ops, SparseCore 0:
  563.2 71.7 reduce-scatter.1
